TPU v7x, 32 devices: a whole 2x2x4 slice. The times are simulated.
32 devices in a mesh: row: 4 (over y, x), bus: 8 (over z, core).
Axes of the slice: x: 2, y: 2, z: 4, core: 2. Of those that a mesh axis runs over, the one named last changes fastest.
Arguments:
- monitored: bfloat16 [512, 32768], P('row', 'bus'), may hold values from -6 to 6
- outaged: bfloat16 [256, 32768], P('row', 'bus'), may hold values from -6 to 6
- bus_weight: float32 [32768], P('bus'), may hold values from 0.5 to 4
- lodf_table: float32 [1024], replicated, may hold values from -1.5 to 1.5
- mon_id: int32 [2048], P('row'), may hold values from 0 to 511
- out_id: int32 [2048], P('row'), may hold values from 0 to 255
- lodf_idx: int32 [2048], P('row'), may hold values from 0 to 1023
Outputs:
- gram: float32 [2048, 2048], P('row', 'bus')
All inputs are finite; a program needn't handle non-finite values.
Results may differ from a plain program's by a relative error of at most 0.0007.
Values may be sent and summed in bfloat16 or wider, within the bound.
A program may use at most 128 MiB of HBM per device.

v0:
```python
import jax
import jax.numpy as jnp
from jax import lax
from jax.sharding import PartitionSpec as P

NB = 32768


def build_rows(mon_rows, out_rows, lodf_table, mon_id, out_id, lodf_idx):
    entries = jnp.arange(lodf_table.shape[0], dtype=jnp.int32)
    coeff = jnp.sum(
        jnp.where(lodf_idx[:, None] == entries[None, :], lodf_table[None, :], 0.0), axis=1
    )
    base = jnp.take(mon_rows, mon_id, axis=0).astype(jnp.float32)
    extra = jnp.take(out_rows, out_id, axis=0).astype(jnp.float32)
    return (base + coeff[:, None] * extra).astype(jnp.bfloat16)


def local(monitored, outaged, bus_weight, lodf_table, mon_id, out_id, lodf_idx):
    mon_rows, out_rows = (
        lax.all_gather(monitored, "row", axis=0, tiled=True),
        lax.all_gather(outaged, "row", axis=0, tiled=True),
    )
    scaling = bus_weight / NB
    mon_all, out_all, lodf_all = (
        lax.all_gather(mon_id, "row", axis=0, tiled=True),
        lax.all_gather(out_id, "row", axis=0, tiled=True),
        lax.all_gather(lodf_idx, "row", axis=0, tiled=True),
    )
    post_all = build_rows(mon_rows, out_rows, lodf_table, mon_all, out_all, lodf_all)
    weighted_all = (post_all.astype(jnp.float32) * scaling[None, :]).astype(jnp.bfloat16)
    local_rows = mon_id.shape[0]
    offset = lax.axis_index("row") * local_rows
    post_local = lax.dynamic_slice_in_dim(post_all, offset, local_rows, 0)
    transposed = lax.psum_scatter(
        lax.dot_general(
            weighted_all, post_local, (((1,), (1,)), ((), ())), preferred_element_type=jnp.float32
        ),
        "bus",
        scatter_dimension=0,
        tiled=True,
    )
    return transposed.T


def solution(mesh):
    in_specs = (P("row", "bus"), P("row", "bus"), P("bus"), P(), P("row"), P("row"), P("row"))
    out_specs = P("row", "bus")
    return jax.shard_map(local, mesh=mesh, in_specs=in_specs, out_specs=out_specs, check_vma=False)
```

profile of v0, /device:TPU:0, one launch (start us, length us, event | category | flops | bytes accessed | tf_op | source)
XLA Modules:
  0.0 230.6 jit_solution(17686515446069697763)
XLA Ops:
  6.5 0.0 all-gather.8.cloned.1.call-start
  6.5 0.7 all-gather.8.cloned.1.call-update
  7.3 0.0 all-gather.6.cloned.1.call-start
  7.3 0.7 all-gather.6.cloned.1.call-update
  8.0 0.0 reduce-scatter.2.cloned.1.call-start
  8.1 9.7 %all-gather = s32[4,1,512]{2,1,0:T(1,128)S(1)} all-gather(s32[1,1,512]{2,1,0:T(1,128)} %bitcast.13), channel_id=1, replica_groups=mesh['row'=4,'bus'=8] {'row'}, dimensions={0}, use_global_device_ids=true | all-gather | bytes 10240 | tf_op jit(solution)/shard_map/all_gather | solution.py:26
  17.8 8.2 %all-gather.2 = s32[4,1,512]{2,1,0:T(1,128)S(1)} all-gather(s32[1,1,512]{2,1,0:T(1,128)} %bitcast.14), channel_id=1, replica_groups=mesh['row'=4,'bus'=8] {'row'}, dimensions={0}, use_global_device_ids=true | all-gather | bytes 10240 | tf_op jit(solution)/shard_map/all_gather | solution.py:27
  25.9 7.2 %all-gather.1 = s32[4,1,512]{2,1,0:T(1,128)S(1)} all-gather(s32[1,1,512]{2,1,0:T(1,128)} %bitcast.15), channel_id=1, replica_groups=mesh['row'=4,'bus'=8] {'row'}, dimensions={0}, use_global_device_ids=true | all-gather | bytes 10240 | tf_op jit(solution)/shard_map/all_gather | solution.py:28
  33.2 0.7 broadcast_multiply_fusion
  34.0 2.0 select_reduce_fusion
  36.0 11.2 %all-gather.8.cloned.1.call-done = bf16[256,4096]{1,0:T(8,128)(2,1)} async-done(((bf16[64,4096]{1,0:T(8,128)(2,1)}), bf16[256,4096]{1,0:T(8,128)(2,1)}) %all-gather.8.cloned.1.call-update) | async-done | bytes 2097168 | tf_op jit(solution)/shard_map/all_gather | solution.py:22
  47.2 30.5 %gather_fusion.1 = bf16[2048,4096]{1,0:T(8,128)(2,1)} fusion(bf16[256,4096]{1,0:T(8,128)(2,1)} %all-gather.8.cloned.1.call-done, s32[2048]{0:T(1024)S(1)} %fusion.4), kind=kCustom, calls=%fused_computation.1 | custom fusion | bytes 33562624 | tf_op jit(solution)/shard_map/jit(_take)/gather | solution.py:15
  77.7 23.9 %all-gather.6.cloned.1.call-done = bf16[512,4096]{1,0:T(8,128)(2,1)} async-done(((bf16[128,4096]{1,0:T(8,128)(2,1)}), bf16[512,4096]{1,0:T(8,128)(2,1)}) %all-gather.6.cloned.1.call-update) | async-done | bytes 4194320 | tf_op jit(solution)/shard_map/all_gather | solution.py:21
  101.6 31.4 %gather_fusion = bf16[2048,4096]{1,0:T(8,128)(2,1)} fusion(bf16[512,4096]{1,0:T(8,128)(2,1)} %all-gather.6.cloned.1.call-done, s32[2048]{0:T(1024)S(1)} %fusion.3), kind=kCustom, calls=%fused_computation | custom fusion | bytes 33562624 | tf_op jit(solution)/shard_map/jit(_take)/gather | solution.py:14
  133.0 22.8 %add_convert_fusion = bf16[2048,4096]{1,0:T(8,128)(2,1)} fusion(bf16[2048,4096]{1,0:T(8,128)(2,1)} %gather_fusion.1, f32[2048]{0:T(1024)S(1)} %select_reduce_fusion, bf16[2048,4096]{1,0:T(8,128)(2,1)} %gather_fusion, pred[2048]{0:T(1024)(128)(4,1)S(1)} %compare_and_fusion, pred[2048]{0:T(1024)(128)(4,1)S(1)} %compare_and_fusion.1), kind=kLoop, calls=%fused_computation.3 | loop fusion | flops 58720256 | bytes 50343936 | tf_op jit(solution)/shard_map/convert_element_type | solution.py:16
  155.8 17.0 %fusion = f32[2048,512]{1,0:T(8,128)} fusion(bf16[2048,4096]{1,0:T(8,128)(2,1)} %add_convert_fusion, f32[4096]{0:T(1024)S(1)} %broadcast_multiply_fusion, s32[]{:T(128)S(6)} %select_n.29), kind=kOutput, calls=%fused_computation.4 | convolution fusion | flops 8615100416 | bytes 25182212 | tf_op jit(solution)/shard_map/dot_general | solution.py:36
  172.8 0.0 reduce-scatter.2.cloned.1.call-update
  172.8 49.2 %reduce-scatter.2.cloned.1.call-done = f32[256,512]{1,0:T(8,128)} async-done(((f32[2048,512]{1,0:T(8,128)}), f32[256,512]{1,0:T(8,128)}) %reduce-scatter.2.cloned.1.call-update) | async-done | bytes 524304 | tf_op jit(solution)/shard_map/reduce_scatter | solution.py:35
  222.0 2.0 copy.10
  (4 shorter events, 0.0 us)
Async XLA Ops:
  6.5 40.6 %all-gather.8.cloned.1.call-start = ((), (), s32[]{:S(2)}) async-start(), calls=%async_computation.2 | async-start | bytes 2621440 | tf_op jit(solution)/shard_map/all_gather | solution.py:22
  7.3 94.4 %all-gather.6.cloned.1.call-start = ((), (), s32[]{:S(2)}) async-start(), calls=%async_computation.1 | async-start | bytes 5242880 | tf_op jit(solution)/shard_map/all_gather | solution.py:21
  8.0 214.0 %reduce-scatter.2.cloned.1.call-start = ((), (), s32[]{:S(2)}) async-start(), calls=%async_computation.3 | async-start | bytes 4718592 | tf_op jit(solution)/shard_map/reduce_scatter | solution.py:35
Sparse Core Ops, SparseCore 0:
  9.2 37.9 all-gather.7
  49.0 52.5 all-gather.5
  173.0 48.9 reduce-scatter.1
where the time goes:
time: 231 us
  waiting for transfers between devices  85.7 us (37%)
  local copies, waits for them, and re-layouts  63.9 us (28%)
  other arithmetic  25.5 us (11%)
  blocking collectives  25.1 us (11%)
  matrix products  17 us (7%)
  between operations  13.1 us (6%)
    reduce_scatter x1, waiting for transfers between devices, local(): lax.psum_scatter(lax.dot_general(weighted_all, post_local, (((1,), (1,)),...  49.2 us
    gather x1, local copies, waits for them, and re-layouts, build_rows(): base = jnp.take(mon_rows, mon_id, axis=0).astype(jnp.float32)  31.4 us
    gather x1, local copies, waits for them, and re-layouts, build_rows(): extra = jnp.take(out_rows, out_id, axis=0).astype(jnp.float32)  30.5 us
    all_gather x1, waiting for transfers between devices, local(): lax.all_gather(monitored, 'row', axis=0, tiled=True)  23.9 us
    convert_element_type x1, other arithmetic, build_rows(): return (base + coeff[:, None] * extra).astype(jnp.bfloat16)  22.8 us
    dot_general x1, matrix products, local(): lax.dot_general(weighted_all, post_local, (((1,), (1,)), ((), ())), prefe...  17 us
    all_gather x1, waiting for transfers between devices, local(): lax.all_gather(outaged, 'row', axis=0, tiled=True)  11.2 us
    all_gather x1, blocking collectives, local(): lax.all_gather(mon_id, 'row', axis=0, tiled=True)  9.7 us
  transfers between devices with their start and end apart: 3, of which 3 were waited for; matrix products, arithmetic and copies ran while one was open for 14% of the time, Pallas kernels for 0%

commit v1 on v0

v1 whole, which is shorter than its diff:
```python
import functools

import jax
import jax.numpy as jnp
from jax import lax
from jax.experimental import pallas as pl
from jax.experimental.pallas import tpu as pltpu
from jax.sharding import PartitionSpec as P

BLK = 256
F32 = jnp.float32
BF16 = jnp.bfloat16
MESH = pl.DeviceIdType.MESH


def split3(v):
    a = v.astype(BF16)
    rest = v - a.astype(F32)
    b = rest.astype(BF16)
    return a, b, (rest - b.astype(F32)).astype(BF16)


def dot(a, b):
    return jnp.dot(a, b, preferred_element_type=F32)


def dot_t(a, b):
    return lax.dot_general(a, b, (((1,), (1,)), ((), ())), preferred_element_type=F32)


def down(lanes):
    n = lanes.shape[1]
    return jnp.broadcast_to(lanes, (128, n)).T


def factors(idx, table_t, entries):
    n = idx.shape[1]
    parts = []
    for lo in range(0, n, 128):
        total = jnp.zeros((1, 128), F32)
        for e in range(0, entries, 128):
            rows = lax.broadcasted_iota(jnp.int32, (128, 128), 0) + e
            hit = jnp.where(rows == idx[:, lo:lo + 128], table_t[e:e + 128, :], 0.0)
            total = total + jnp.sum(hit, axis=0, keepdims=True)
        parts.append(total)
    return jnp.concatenate(parts, axis=1)


def kernel(dims, mon_ref, out_ref, w_ref, table_ref, mid_ref, oid_ref, lid_ref,
           gram_ref, x, xh, xl, gp, cbuf, gacc, rbuf, gs, zbuf, gz, full, tt, ids,
           brow, x_s, x_r, own, c_s, c_r, r_s, r_r, z_s, z_r, za_s, za_r, ra_s, ra_r, ca_s, ca_r):
    R, B, nb_all = dims
    Z = B // 2
    r = lax.axis_index("row")
    b = lax.axis_index("bus")
    core = lax.rem(b, 2)
    zi = lax.div(b, 2)
    mrows, cols = mon_ref.shape
    orows = out_ref.shape[0]
    nm, no = mrows * R, orows * R
    cq = cols // R
    nblk_m, nblk_o = nm // BLK, no // BLK
    nblk = nblk_m + nblk_o
    kl = mid_ref.shape[1]
    kc = kl * R // B
    H = gp.shape[0] // 2
    hq = H // R
    pz = hq // Z

    barrier = pltpu.get_barrier_semaphore()
    for d in range(1, R):
        pl.semaphore_signal(barrier, inc=1, device_id={"row": lax.rem(r + d, R)}, device_id_type=MESH)
    for d in range(1, Z):
        pl.semaphore_signal(barrier, inc=1, device_id={"bus": lax.rem(zi + d, Z) * 2 + core}, device_id_type=MESH)
    pl.semaphore_signal(barrier, inc=1, device_id={"bus": zi * 2 + (1 - core)}, device_id_type=MESH)
    pl.semaphore_wait(barrier, R - 1 + Z - 1 + 1)

    def quarter(ref, q):
        return ref.at[:, pl.ds(pl.multiple_of(q * cq, 128), cq)]

    mon_dst = x.at[pl.ds(pl.multiple_of(r * mrows, mrows), mrows), :]
    out_dst = x.at[pl.ds(pl.multiple_of(nm + r * orows, orows), orows), :]
    first = []
    for d in range(1, R):
        q = lax.rem(r + d, R)
        pairs = [(quarter(mon_ref, q), mon_dst), (quarter(out_ref, q), out_dst),
                 (mid_ref, ids.at[0, r]), (oid_ref, ids.at[1, r]), (lid_ref, ids.at[2, r])]
        for i, (src, dst) in enumerate(pairs):
            c = pltpu.make_async_remote_copy(
                src_ref=src, dst_ref=dst, send_sem=x_s.at[d - 1, i], recv_sem=x_r.at[d - 1, i],
                device_id={"row": q}, device_id_type=MESH)
            c.start()
            first.append(c)
    mine = [(quarter(mon_ref, r), mon_dst), (quarter(out_ref, r), out_dst),
            (mid_ref, ids.at[0, r]), (oid_ref, ids.at[1, r]), (lid_ref, ids.at[2, r])]
    local = []
    for i, (src, dst) in enumerate(mine):
        c = pltpu.make_async_copy(src, dst, own.at[i])
        c.start()
        local.append(c)

    entries = table_ref.shape[1]
    for e in range(0, entries, 128):
        tt[e:e + 128, :] = down(table_ref[:, e:e + 128])
    c_row = down(factors(lid_ref[...], tt, entries))
    lane = lax.broadcasted_iota(jnp.int32, (kl, 128), 1)
    mid_t = down(mid_ref[...].astype(F32)).astype(jnp.int32)
    for e in range(0, nm, 128):
        brow[:, e:e + 128] = jnp.where(mid_t == lane + e, 1.0, 0.0).astype(BF16)
    oid_t = down(oid_ref[...].astype(F32)).astype(jnp.int32)
    for e in range(0, no, 128):
        brow[:, nm + e:nm + e + 128] = jnp.where(oid_t == lane + e, 1.0, 0.0).astype(BF16)
    scale = w_ref[:, pl.ds(pl.multiple_of(r * cq, 128), cq)] * (1.0 / nb_all)

    for c in local:
        c.wait()
    for c in first:
        c.wait()

    for i in range(nblk):
        rows = slice(i * BLK, (i + 1) * BLK)
        v = x[rows, :].astype(F32) * scale
        h = v.astype(BF16)
        xh[rows, :] = h
        xl[rows, :] = (v - h.astype(F32)).astype(BF16)
    at = {}
    for i in range(nblk):
        for j in range(i, nblk):
            k = len(at)
            at[i, j] = k
            a = x[i * BLK:(i + 1) * BLK, :]
            rows = slice(j * BLK, (j + 1) * BLK)
            gp[k * BLK:(k + 1) * BLK, :] = dot_t(a, xh[rows, :]) + dot_t(a, xl[rows, :])
    if gp.shape[0] > len(at) * BLK:
        gp[len(at) * BLK:, :] = jnp.zeros((gp.shape[0] - len(at) * BLK, BLK), F32)

    other = zi * 2 + (1 - core)
    c = pltpu.make_async_remote_copy(
        src_ref=gp.at[pl.ds(pl.multiple_of((1 - core) * H, 8), H), :], dst_ref=cbuf,
        send_sem=c_s, recv_sem=c_r, device_id={"bus": other}, device_id_type=MESH)
    c.start()
    c.wait()
    gacc[...] = gp[pl.ds(pl.multiple_of(core * H, 8), H), :] + cbuf[...]

    copies = []
    for d in range(1, R):
        q = lax.rem(r + d, R)
        c = pltpu.make_async_remote_copy(
            src_ref=gacc.at[pl.ds(pl.multiple_of(q * hq, 8), hq), :], dst_ref=rbuf.at[d - 1],
            send_sem=r_s.at[d - 1], recv_sem=r_r.at[d - 1], device_id={"row": q}, device_id_type=MESH)
        c.start()
        copies.append(c)
    for c in copies:
        c.wait()
    total = gacc[pl.ds(pl.multiple_of(r * hq, 8), hq), :]
    for d in range(1, R):
        total = total + rbuf[d - 1]
    gs[...] = total

    copies = []
    for d in range(1, Z):
        q = lax.rem(zi + d, Z)
        c = pltpu.make_async_remote_copy(
            src_ref=gs.at[pl.ds(pl.multiple_of(q * pz, 8), pz), :], dst_ref=zbuf.at[d - 1],
            send_sem=z_s.at[d - 1], recv_sem=z_r.at[d - 1],
            device_id={"bus": q * 2 + core}, device_id_type=MESH)
        c.start()
        copies.append(c)
    for c in copies:
        c.wait()
    total = gs[pl.ds(pl.multiple_of(zi * pz, 8), pz), :]
    for d in range(1, Z):
        total = total + zbuf[d - 1]
    gz[...] = total

    start = core * H + r * hq
    piece = full.at[pl.ds(pl.multiple_of(start + zi * pz, 8), pz), :]
    keep = pltpu.make_async_copy(gz, piece, own.at[0])
    keep.start()
    copies = []
    for d in range(1, Z):
        c = pltpu.make_async_remote_copy(
            src_ref=gz, dst_ref=piece, send_sem=za_s.at[d - 1], recv_sem=za_r.at[d - 1],
            device_id={"bus": lax.rem(zi + d, Z) * 2 + core}, device_id_type=MESH)
        c.start()
        copies.append(c)
    keep.wait()
    for c in copies:
        c.wait()
    piece = full.at[pl.ds(pl.multiple_of(start, 8), hq), :]
    copies = []
    for d in range(1, R):
        c = pltpu.make_async_remote_copy(
            src_ref=piece, dst_ref=piece, send_sem=ra_s.at[d - 1], recv_sem=ra_r.at[d - 1],
            device_id={"row": lax.rem(r + d, R)}, device_id_type=MESH)
        c.start()
        copies.append(c)

    owner = lax.div(b * kc, kl)
    begin = pl.multiple_of(lax.rem(b * kc, kl), 128)
    mid_c = ids[0, owner, :, pl.ds(begin, kc)]
    oid_c = ids[1, owner, :, pl.ds(begin, kc)]
    c_col = factors(ids[2, owner, :, pl.ds(begin, kc)], tt, entries)
    sub = lax.broadcasted_iota(jnp.int32, (BLK, kc), 0)
    bcol = [jnp.where(sub + j * BLK == mid_c, 1.0, 0.0).astype(BF16) for j in range(nblk_m)]
    bcol += [jnp.where(sub + j * BLK == oid_c, 1.0, 0.0).astype(BF16) for j in range(nblk_o)]

    for c in copies:
        c.wait()
    piece = full.at[pl.ds(pl.multiple_of(core * H, 8), H), :]
    c = pltpu.make_async_remote_copy(
        src_ref=piece, dst_ref=piece, send_sem=ca_s, recv_sem=ca_r,
        device_id={"bus": other}, device_id_type=MESH)
    c.start()
    c.wait()

    t_m = [jnp.zeros((BLK, kc), F32) for _ in range(nblk)]
    t_o = [jnp.zeros((BLK, kc), F32) for _ in range(nblk)]
    for (i, j), k in at.items():
        g = full[k * BLK:(k + 1) * BLK, :]
        for to, frm, part in ((i, j, g), (j, i, g.T)) if i != j else ((i, j, g),):
            here = t_m if frm < nblk_m else t_o
            for p in split3(part):
                here[to] = here[to] + dot(p, bcol[frm])
    g_m = jnp.zeros((kl, kc), F32)
    g_o = jnp.zeros((kl, kc), F32)
    for i in range(nblk):
        s = brow[:, i * BLK:(i + 1) * BLK]
        acc = jnp.zeros((kl, kc), F32)
        for p in split3(t_m[i] + t_o[i] * c_col):
            acc = acc + dot(s, p)
        if i < nblk_m:
            g_m = g_m + acc
        else:
            g_o = g_o + acc
    gram_ref[...] = g_m + g_o * jnp.concatenate([c_row] * (kc // 128), axis=1)


def solution(mesh):
    R, B = mesh.shape["row"], mesh.shape["bus"]
    Z = B // 2

    def local(monitored, outaged, bus_weight, lodf_table, mon_id, out_id, lodf_idx):
        mrows, cols = monitored.shape
        orows = outaged.shape[0]
        n = (mrows + orows) * R
        cq = cols // R
        nblk = n // BLK
        kl = mon_id.shape[0]
        kc = kl * R // B
        unit = 8 * R * B
        packed = -(-(nblk * (nblk + 1) // 2 * BLK) // unit) * unit
        H = packed // 2
        hq = H // R
        pz = hq // Z
        vmem = pl.BlockSpec(memory_space=pltpu.VMEM)
        hbm = pl.BlockSpec(memory_space=pl.ANY)
        dma = pltpu.SemaphoreType.DMA
        return pl.pallas_call(
            functools.partial(kernel, (R, B, cols * B)),
            out_shape=jax.ShapeDtypeStruct((kl, kc), F32),
            in_specs=[hbm, hbm] + [vmem] * 5,
            out_specs=vmem,
            scratch_shapes=[
                pltpu.VMEM((n, cq), BF16),
                pltpu.VMEM((n, cq), BF16),
                pltpu.VMEM((n, cq), BF16),
                pltpu.VMEM((packed, BLK), F32),
                pltpu.VMEM((H, BLK), F32),
                pltpu.VMEM((H, BLK), F32),
                pltpu.VMEM((R - 1, hq, BLK), F32),
                pltpu.VMEM((hq, BLK), F32),
                pltpu.VMEM((Z - 1, pz, BLK), F32),
                pltpu.VMEM((pz, BLK), F32),
                pltpu.VMEM((packed, BLK), F32),
                pltpu.VMEM((lodf_table.shape[0], 128), F32),
                pltpu.VMEM((3, R, 1, kl), jnp.int32),
                pltpu.VMEM((kl, n), BF16),
                dma((R - 1, 5)), dma((R - 1, 5)), dma((5,)),
                dma, dma,
                dma((R - 1,)), dma((R - 1,)),
                dma((Z - 1,)), dma((Z - 1,)),
                dma((Z - 1,)), dma((Z - 1,)),
                dma((R - 1,)), dma((R - 1,)),
                dma, dma,
            ],
            compiler_params=pltpu.CompilerParams(
                collective_id=0, has_side_effects=True, vmem_limit_bytes=60 * 1024 * 1024),
        )(monitored, outaged, bus_weight[None, :], lodf_table[None, :],
          mon_id[None, :], out_id[None, :], lodf_idx[None, :])

    in_specs = (P("row", "bus"), P("row", "bus"), P("bus"), P(), P("row"), P("row"), P("row"))
    return jax.shard_map(local, mesh=mesh, in_specs=in_specs, out_specs=P("row", "bus"), check_vma=False)
```

time: 231 us -> 66 us (0.29)
  waiting for transfers between devices: 85.7 us -> 0 us
  Pallas kernels: 0 us -> 63.9 us
  local copies, waits for them, and re-layouts: 63.9 us -> 1.87 us
  other arithmetic: 25.5 us -> 0 us
  blocking collectives: 25.1 us -> 0 us
  matrix products: 17 us -> 0 us
  between operations: 13.1 us -> 0.01 us
    pallas_call x0 -> x1, Pallas kernels: none -> 63.9 us  [local(): pl.pallas_call(functools.partial(kernel, (R, B, cols * B)), out_shape=jax...]
    gather x2 -> x0, local copies, waits for them, and re-layouts: 61.9 us -> none  [the longest x1 31.4 us: build_rows(): base = jnp.take(mon_rows, mon_id, axis=0).astype(jnp.float32)]
    reduce_scatter x1 -> x0, waiting for transfers between devices: 49.2 us -> none  [local(): lax.psum_scatter(lax.dot_general(weighted_all, post_local, (((1,), (1,)),...]
    all_gather x2 -> x0, waiting for transfers between devices: 35.2 us -> none  [the longest x1 23.9 us: local(): lax.all_gather(monitored, 'row', axis=0, tiled=True)]
    all_gather x3 -> x0, blocking collectives: 25.1 us -> none  [the longest x1 9.7 us: local(): lax.all_gather(mon_id, 'row', axis=0, tiled=True)]
    convert_element_type x1 -> x0, other arithmetic: 22.8 us -> none  [build_rows(): return (base + coeff[:, None] * extra).astype(jnp.bfloat16)]
    dot_general x1 -> x0, matrix products: 17 us -> none  [local(): lax.dot_general(weighted_all, post_local, (((1,), (1,)), ((), ())), prefe...]
  transfers between devices with their start and end apart: 3 -> 0, of which waited for: 3 -> 0; matrix products, arithmetic and copies ran while one was open for 14% -> 0% of each run, Pallas kernels for 0% -> 0%
where the time goes in v1:
time: 66 us; the launch traced here: 65.8 us
  Pallas kernels  63.9 us (97%)
  local copies, waits for them, and re-layouts  1.87 us (3%)
    pallas_call x1, Pallas kernels, local(): pl.pallas_call(functools.partial(kernel, (R, B, cols * B)), out_shape=jax...  63.9 us
    unnamed x1, local copies, waits for them, and re-layouts  1.87 us

profile of v1, /device:TPU:0, one launch (start us, length us, event | category | flops | bytes accessed | tf_op | source)
XLA Modules:
  0.0 65.8 jit_solution(8260987124822087394)
XLA Ops:
  0.0 63.9 %shard_map.73 = f32[512,256]{1,0:T(8,128)} custom-call(bf16[128,4096]{1,0:T(8,128)(2,1)} %mon_ref.1, bf16[64,4096]{1,0:T(8,128)(2,1)} %out_ref.1, f32[1,4096]{1,0:T(1,128)} %bitcast.5, f32[1,1024]{1,0:T(1,128)} %bitcast.6, s32[1,512]{1,0:T(1,128)} %bitcast.7, s32[1,512]{1,0:T(1,128)} %bitcast.8, s32[1,512]{1,0:T(1,128)} %bitcast.9), custom_call_target="tpu_custom_call" | custom-call | tf_op jit(solution)/shard_map/pallas_call | solution.py:259
  63.9 1.9 %copy.9 = f32[512,256]{1,0:T(8,128)} copy(f32[512,256]{1,0:T(8,128)} %shard_map.73) | data formatting | bytes 1048576

commit v2 on v0

v2 whole, which is shorter than its diff:
```python
import functools

import jax
import jax.numpy as jnp
from jax import lax
from jax.experimental import pallas as pl
from jax.experimental.pallas import tpu as pltpu
from jax.sharding import PartitionSpec as P

BLK = 256
F32 = jnp.float32
BF16 = jnp.bfloat16
MESH = pl.DeviceIdType.MESH


def split3(v):
    a = v.astype(BF16)
    rest = v - a.astype(F32)
    b = rest.astype(BF16)
    return a, b, (rest - b.astype(F32)).astype(BF16)


def dot(a, b):
    return jnp.dot(a, b, preferred_element_type=F32)


def dot_t(a, b):
    return lax.dot_general(a, b, (((1,), (1,)), ((), ())), preferred_element_type=F32)


def down(lanes):
    n = lanes.shape[1]
    return jnp.broadcast_to(lanes, (128, n)).T


def factors(idx, table_t, entries):
    n = idx.shape[1]
    parts = []
    for lo in range(0, n, 128):
        total = jnp.zeros((1, 128), F32)
        for e in range(0, entries, 128):
            rows = lax.broadcasted_iota(jnp.int32, (128, 128), 0) + e
            hit = jnp.where(rows == idx[:, lo:lo + 128], table_t[e:e + 128, :], 0.0)
            total = total + jnp.sum(hit, axis=0, keepdims=True)
        parts.append(total)
    return jnp.concatenate(parts, axis=1)


class Stream:
    def __init__(self, refs, blocks, me, core, other, axes):
        (self.gp, self.cbuf, self.acc, self.b1, self.s1, self.b2, self.full,
         self.cs, self.cr, self.p1s, self.p1r, self.p2s, self.p2r,
         self.a1s, self.a1r, self.a2s, self.a2r, self.ds, self.dr) = refs
        self.blocks = blocks
        self.core, self.other = core, other
        (self.n1, self.i1, self.dev1), (self.n2, self.i2, self.dev2) = axes
        self.H = self.gp.shape[0] // 2
        self.h1 = self.H // self.n1
        self.pz = self.h1 // self.n2
        self.z_first = me

    def compute(self, x, xh, xl):
        for k, (i, j) in enumerate(self.blocks):
            left = x[i * BLK:(i + 1) * BLK, :]
            rows = slice(j * BLK, (j + 1) * BLK)
            self.gp[k * BLK:(k + 1) * BLK, :] = dot_t(left, xh[rows, :]) + dot_t(left, xl[rows, :])
        used = len(self.blocks) * BLK
        if self.gp.shape[0] > used:
            self.gp[used:, :] = jnp.zeros((self.gp.shape[0] - used, BLK), F32)

    def rows(self, start, count):
        return pl.ds(pl.multiple_of(start, 8), count)

    def send(self, src, dst, s, r, dev):
        c = pltpu.make_async_remote_copy(
            src_ref=src, dst_ref=dst, send_sem=s, recv_sem=r, device_id=dev, device_id_type=MESH)
        c.start()
        return c

    def pair_start(self):
        self.c = [self.send(self.gp.at[self.rows((1 - self.core) * self.H, self.H), :], self.cbuf,
                            self.cs, self.cr, self.other)]

    def wait(self):
        for c in self.c:
            c.wait()

    def one_start(self):
        self.wait()
        self.acc[...] = self.gp[self.rows(self.core * self.H, self.H), :] + self.cbuf[...]
        self.c = []
        for d in range(1, self.n1):
            q = lax.rem(self.i1 + d, self.n1)
            self.c.append(self.send(self.acc.at[self.rows(q * self.h1, self.h1), :], self.b1.at[d - 1],
                                    self.p1s.at[d - 1], self.p1r.at[d - 1], self.dev1(q)))

    def two_start(self):
        self.wait()
        total = self.acc[self.rows(self.i1 * self.h1, self.h1), :]
        for d in range(1, self.n1):
            total = total + self.b1[d - 1]
        self.s1[...] = total
        self.c = []
        for d in range(1, self.n2):
            q = lax.rem(self.i2 + d, self.n2)
            self.c.append(self.send(self.s1.at[self.rows(q * self.pz, self.pz), :], self.b2.at[d - 1],
                                    self.p2s.at[d - 1], self.p2r.at[d - 1], self.dev2(q)))

    def piece(self, z, r):
        i1, i2 = (z, r) if self.z_first else (r, z)
        return self.rows(self.core * self.H + i1 * self.h1 + i2 * self.pz, self.pz)

    def back_start(self):
        self.wait()
        total = self.s1[self.rows(self.i2 * self.pz, self.pz), :]
        for d in range(1, self.n2):
            total = total + self.b2[d - 1]
        if self.z_first:
            self.Z, self.zi, self.zdev = self.n1, self.i1, self.dev1
            self.R, self.r, self.rdev = self.n2, self.i2, self.dev2
        else:
            self.Z, self.zi, self.zdev = self.n2, self.i2, self.dev2
            self.R, self.r, self.rdev = self.n1, self.i1, self.dev1
        at = self.piece(self.zi, self.r)
        self.full[at, :] = total
        ref = self.full.at[at, :]
        self.zc = []
        for d in range(1, self.Z):
            self.zc.append(self.send(ref, ref, self.a1s.at[d - 1], self.a1r.at[d - 1],
                                     self.zdev(lax.rem(self.zi + d, self.Z))))
        self.c = []
        self.spread(0)

    def spread(self, e):
        ref = self.full.at[self.piece(lax.rem(self.zi + self.Z - e, self.Z), self.r), :]
        for d in range(1, self.R):
            self.c.append(self.send(ref, ref, self.a2s.at[e, d - 1], self.a2r.at[e, d - 1],
                                    self.rdev(lax.rem(self.r + d, self.R))))

    def spread_rest(self):
        for e in range(1, self.Z):
            self.zc[e - 1].wait()
            self.spread(e)

    def pair_back(self):
        self.wait()
        ref = self.full.at[self.rows(self.core * self.H, self.H), :]
        self.c = [self.send(ref, ref, self.ds, self.dr, self.other)]


def select(ids, block, rows_each, dev_rows, axis, shape):
    p = lax.broadcasted_iota(jnp.int32, shape, axis)
    if axis == 1:
        p = p + block[1]
    shift = rows_each.bit_length() - 1
    line = lax.shift_right_logical(p, jnp.full(shape, shift, jnp.int32)) * (dev_rows - rows_each) + p
    return jnp.where(ids == line + block[0] * rows_each, 1.0, 0.0).astype(BF16)


def kernel(dims, mon_ref, out_ref, w_ref, table_ref, mid_ref, oid_ref, lid_ref,
           gram_ref, x, xh, xl, tt, ids, brow, x_s, x_r, i_s, i_r, own, own_i, *rest):
    R, B, nb_all = dims
    Z = B // 2
    r = lax.axis_index("row")
    b = lax.axis_index("bus")
    core = lax.rem(b, 2)
    zi = lax.div(b, 2)
    mrows, cols = mon_ref.shape
    orows = out_ref.shape[0]
    each = BLK // R
    cq = cols // R
    nblk_o, nblk_m = orows // each, mrows // each
    nblk = nblk_m + nblk_o
    kl = mid_ref.shape[1]
    kc = kl * R // B

    def row_dev(q):
        return {"row": q}

    def z_dev(q):
        return {"bus": q * 2 + core}

    pair_dev = {"bus": zi * 2 + (1 - core)}
    barrier = pltpu.get_barrier_semaphore()
    for d in range(1, R):
        pl.semaphore_signal(barrier, inc=1, device_id=row_dev(lax.rem(r + d, R)), device_id_type=MESH)
    for d in range(1, Z):
        pl.semaphore_signal(barrier, inc=1, device_id=z_dev(lax.rem(zi + d, Z)), device_id_type=MESH)
    pl.semaphore_signal(barrier, inc=1, device_id=pair_dev, device_id_type=MESH)
    pl.semaphore_wait(barrier, R - 1 + Z - 1 + 1)

    def source(k, q):
        ref, k = (out_ref, k) if k < nblk_o else (mon_ref, k - nblk_o)
        return ref.at[k * each:(k + 1) * each, pl.ds(pl.multiple_of(q * cq, 128), cq)]

    def target(k):
        return x.at[pl.ds(pl.multiple_of(k * BLK + r * each, each), each), :]

    chunks = []
    for k in range(nblk):
        chunk = []
        for d in range(1, R):
            q = lax.rem(r + d, R)
            c = pltpu.make_async_remote_copy(
                src_ref=source(k, q), dst_ref=target(k), send_sem=x_s.at[d - 1, k], recv_sem=x_r.at[d - 1, k],
                device_id=row_dev(q), device_id_type=MESH)
            c.start()
            chunk.append(c)
        c = pltpu.make_async_copy(source(k, r), target(k), own.at[k])
        c.start()
        chunk.append(c)
        chunks.append(chunk)
    id_copies = []
    for i, src in enumerate((mid_ref, oid_ref, lid_ref)):
        for d in range(1, R):
            c = pltpu.make_async_remote_copy(
                src_ref=src, dst_ref=ids.at[i, r], send_sem=i_s.at[i, d - 1], recv_sem=i_r.at[i, d - 1],
                device_id=row_dev(lax.rem(r + d, R)), device_id_type=MESH)
            c.start()
            id_copies.append(c)
        c = pltpu.make_async_copy(src, ids.at[i, r], own_i.at[i])
        c.start()
        id_copies.append(c)

    entries = table_ref.shape[1]
    for e in range(0, entries, 128):
        tt[e:e + 128, :] = down(table_ref[:, e:e + 128])
    c_row = down(factors(lid_ref[...], tt, entries))
    oid_t = down(oid_ref[...].astype(F32)).astype(jnp.int32)
    mid_t = down(mid_ref[...].astype(F32)).astype(jnp.int32)
    for k in range(nblk):
        for e in range(0, BLK, 128):
            at = slice(k * BLK + e, k * BLK + e + 128)
            if k < nblk_o:
                brow[:, at] = select(oid_t, (k, e), each, orows, 1, (kl, 128))
            else:
                brow[:, at] = select(mid_t, (k - nblk_o, e), each, mrows, 1, (kl, 128))
    scale = w_ref[:, pl.ds(pl.multiple_of(r * cq, 128), cq)] * (1.0 / nb_all)

    n = len(rest) // 2
    last = nblk - 1
    ab = Stream(rest[:n], [(i, j) for i in range(last) for j in range(i, last)], True, core, pair_dev,
                ((Z, zi, z_dev), (R, r, row_dev)))
    bb = Stream(rest[n:], [(i, last) for i in range(nblk)], False, core, pair_dev,
                ((R, r, row_dev), (Z, zi, z_dev)))

    def arrive(k):
        for c in chunks[k]:
            c.wait()
        rows = slice(k * BLK, (k + 1) * BLK)
        v = x[rows, :].astype(F32) * scale
        h = v.astype(BF16)
        xh[rows, :] = h
        xl[rows, :] = (v - h.astype(F32)).astype(BF16)

    for k in range(last):
        arrive(k)
    ab.compute(x, xh, xl)
    ab.pair_start()
    ab.one_start()
    arrive(last)
    bb.compute(x, xh, xl)
    bb.pair_start()
    bb.one_start()
    ab.two_start()
    bb.two_start()
    ab.back_start()
    bb.back_start()
    ab.spread_rest()

    for c in id_copies:
        c.wait()
    owner = lax.div(b * kc, kl)
    begin = pl.multiple_of(lax.rem(b * kc, kl), 128)
    mid_c = ids[0, owner, :, pl.ds(begin, kc)]
    oid_c = ids[1, owner, :, pl.ds(begin, kc)]
    c_col = factors(ids[2, owner, :, pl.ds(begin, kc)], tt, entries)
    bcol = [select(oid_c, (k, 0), each, orows, 0, (BLK, kc)) for k in range(nblk_o)]
    bcol += [select(mid_c, (k, 0), each, mrows, 0, (BLK, kc)) for k in range(nblk_m)]

    t_m = [jnp.zeros((BLK, kc), F32) for _ in range(nblk)]
    t_o = [jnp.zeros((BLK, kc), F32) for _ in range(nblk)]

    def gather(stream):
        stream.wait()
        for k, (i, j) in enumerate(stream.blocks):
            g = stream.full[k * BLK:(k + 1) * BLK, :]
            for to, frm, part in ((i, j, g), (j, i, g.T)) if i != j else ((i, j, g),):
                here = t_o if frm < nblk_o else t_m
                for p in split3(part):
                    here[to] = here[to] + dot(p, bcol[frm])

    bb.spread_rest()
    ab.pair_back()
    gather(ab)
    bb.pair_back()
    gather(bb)
    g_m = jnp.zeros((kl, kc), F32)
    g_o = jnp.zeros((kl, kc), F32)
    for i in range(nblk):
        s = brow[:, i * BLK:(i + 1) * BLK]
        acc = jnp.zeros((kl, kc), F32)
        for p in split3(t_m[i] + t_o[i] * c_col):
            acc = acc + dot(s, p)
        if i < nblk_o:
            g_o = g_o + acc
        else:
            g_m = g_m + acc
    gram_ref[...] = g_m + g_o * jnp.concatenate([c_row] * (kc // 128), axis=1)


def solution(mesh):
    R, B = mesh.shape["row"], mesh.shape["bus"]
    Z = B // 2

    def stream_scratch(blocks, n1, n2):
        unit = 8 * R * B
        packed = -(-(blocks * BLK) // unit) * unit
        H = packed // 2
        h1 = H // n1
        pz = h1 // n2
        dma = pltpu.SemaphoreType.DMA
        return [
            pltpu.VMEM((packed, BLK), F32),
            pltpu.VMEM((H, BLK), F32),
            pltpu.VMEM((H, BLK), F32),
            pltpu.VMEM((n1 - 1, h1, BLK), F32),
            pltpu.VMEM((h1, BLK), F32),
            pltpu.VMEM((n2 - 1, pz, BLK), F32),
            pltpu.VMEM((packed, BLK), F32),
            dma, dma,
            dma((n1 - 1,)), dma((n1 - 1,)),
            dma((n2 - 1,)), dma((n2 - 1,)),
            dma((Z - 1,)), dma((Z - 1,)),
            dma((Z, R - 1)), dma((Z, R - 1)),
            dma, dma,
        ]

    def local(monitored, outaged, bus_weight, lodf_table, mon_id, out_id, lodf_idx):
        mrows, cols = monitored.shape
        orows = outaged.shape[0]
        n = (mrows + orows) * R
        cq = cols // R
        nblk = n // BLK
        kl = mon_id.shape[0]
        kc = kl * R // B
        vmem = pl.BlockSpec(memory_space=pltpu.VMEM)
        hbm = pl.BlockSpec(memory_space=pl.ANY)
        dma = pltpu.SemaphoreType.DMA
        return pl.pallas_call(
            functools.partial(kernel, (R, B, cols * B)),
            out_shape=jax.ShapeDtypeStruct((kl, kc), F32),
            in_specs=[hbm, hbm] + [vmem] * 5,
            out_specs=vmem,
            scratch_shapes=[
                pltpu.VMEM((n, cq), BF16),
                pltpu.VMEM((n, cq), BF16),
                pltpu.VMEM((n, cq), BF16),
                pltpu.VMEM((lodf_table.shape[0], 128), F32),
                pltpu.VMEM((3, R, 1, kl), jnp.int32),
                pltpu.VMEM((kl, n), BF16),
                dma((R - 1, nblk)), dma((R - 1, nblk)),
                dma((3, R - 1)), dma((3, R - 1)),
                dma((nblk,)), dma((3,)),
            ] + stream_scratch(nblk * (nblk - 1) // 2, Z, R) + stream_scratch(nblk, R, Z),
            compiler_params=pltpu.CompilerParams(
                collective_id=0, has_side_effects=True, vmem_limit_bytes=60 * 1024 * 1024),
        )(monitored, outaged, bus_weight[None, :], lodf_table[None, :],
          mon_id[None, :], out_id[None, :], lodf_idx[None, :])

    in_specs = (P("row", "bus"), P("row", "bus"), P("bus"), P(), P("row"), P("row"), P("row"))
    return jax.shard_map(local, mesh=mesh, in_specs=in_specs, out_specs=P("row", "bus"), check_vma=False)
```

time: 231 us -> 55.9 us (0.24)
  waiting for transfers between devices: 85.7 us -> 0 us
  local copies, waits for them, and re-layouts: 63.9 us -> 1.87 us
  Pallas kernels: 0 us -> 53.8 us
  other arithmetic: 25.5 us -> 0 us
  blocking collectives: 25.1 us -> 0 us
  matrix products: 17 us -> 0 us
  between operations: 13.1 us -> 0.01 us
    gather x2 -> x0, local copies, waits for them, and re-layouts: 61.9 us -> none  [the longest x1 31.4 us: build_rows(): base = jnp.take(mon_rows, mon_id, axis=0).astype(jnp.float32)]
    pallas_call x0 -> x1, Pallas kernels: none -> 53.8 us  [local(): pl.pallas_call(functools.partial(kernel, (R, B, cols * B)), out_shape=jax...]
    reduce_scatter x1 -> x0, waiting for transfers between devices: 49.2 us -> none  [local(): lax.psum_scatter(lax.dot_general(weighted_all, post_local, (((1,), (1,)),...]
    all_gather x2 -> x0, waiting for transfers between devices: 35.2 us -> none  [the longest x1 23.9 us: local(): lax.all_gather(monitored, 'row', axis=0, tiled=True)]
    all_gather x3 -> x0, blocking collectives: 25.1 us -> none  [the longest x1 9.7 us: local(): lax.all_gather(mon_id, 'row', axis=0, tiled=True)]
    convert_element_type x1 -> x0, other arithmetic: 22.8 us -> none  [build_rows(): return (base + coeff[:, None] * extra).astype(jnp.bfloat16)]
    dot_general x1 -> x0, matrix products: 17 us -> none  [local(): lax.dot_general(weighted_all, post_local, (((1,), (1,)), ((), ())), prefe...]
  transfers between devices with their start and end apart: 3 -> 0, of which waited for: 3 -> 0; matrix products, arithmetic and copies ran while one was open for 14% -> 0% of each run, Pallas kernels for 0% -> 0%
where the time goes in v2:
time: 55.9 us; the launch traced here: 55.7 us
  Pallas kernels  53.8 us (96%)
  local copies, waits for them, and re-layouts  1.87 us (3%)
    pallas_call x1, Pallas kernels, local(): pl.pallas_call(functools.partial(kernel, (R, B, cols * B)), out_shape=jax...  53.8 us
    unnamed x1, local copies, waits for them, and re-layouts  1.87 us

profile of v2, /device:TPU:0, one launch (start us, length us, event | category | flops | bytes accessed | tf_op | source)
XLA Modules:
  0.0 55.7 jit_solution(10057646039549669959)
XLA Ops:
  0.0 53.8 %shard_map.73 = f32[512,256]{1,0:T(8,128)} custom-call(bf16[128,4096]{1,0:T(8,128)(2,1)} %mon_ref.1, bf16[64,4096]{1,0:T(8,128)(2,1)} %out_ref.1, f32[1,4096]{1,0:T(1,128)} %bitcast.5, f32[1,1024]{1,0:T(1,128)} %bitcast.6, s32[1,512]{1,0:T(1,128)} %bitcast.7, s32[1,512]{1,0:T(1,128)} %bitcast.8, s32[1,512]{1,0:T(1,128)} %bitcast.9), custom_call_target="tpu_custom_call" | custom-call | tf_op jit(solution)/shard_map/pallas_call | solution.py:350
  53.8 1.9 %copy.9 = f32[512,256]{1,0:T(8,128)} copy(f32[512,256]{1,0:T(8,128)} %shard_map.73) | data formatting | bytes 1048576

commit v3 on v2

--- a/solution.py
+++ b/solution.py
@@ -7,7 +7,7 @@
 from jax.experimental.pallas import tpu as pltpu
 from jax.sharding import PartitionSpec as P
 
-BLK = 256
+BLK = 128
 F32 = jnp.float32
 BF16 = jnp.bfloat16
 MESH = pl.DeviceIdType.MESH
@@ -59,14 +59,15 @@
         self.pz = self.h1 // self.n2
         self.z_first = me
 
-    def compute(self, x, xh, xl):
-        for k, (i, j) in enumerate(self.blocks):
-            left = x[i * BLK:(i + 1) * BLK, :]
-            rows = slice(j * BLK, (j + 1) * BLK)
-            self.gp[k * BLK:(k + 1) * BLK, :] = dot_t(left, xh[rows, :]) + dot_t(left, xl[rows, :])
-        used = len(self.blocks) * BLK
-        if self.gp.shape[0] > used:
-            self.gp[used:, :] = jnp.zeros((self.gp.shape[0] - used, BLK), F32)
+    def compute(self, x, xw):
+        at = 0
+        for k in self.blocks:
+            m = (k + 1) * BLK
+            both = dot_t(x[:m, :], xw[k])
+            self.gp[at:at + m, :] = both[:, :BLK] + both[:, BLK:]
+            at += m
+        if self.gp.shape[0] > at:
+            self.gp[at:, :] = jnp.zeros((self.gp.shape[0] - at, BLK), F32)
 
     def rows(self, start, count):
         return pl.ds(pl.multiple_of(start, 8), count)
@@ -158,7 +159,7 @@
 
 
 def kernel(dims, mon_ref, out_ref, w_ref, table_ref, mid_ref, oid_ref, lid_ref,
-           gram_ref, x, xh, xl, tt, ids, brow, x_s, x_r, i_s, i_r, own, own_i, *rest):
+           gram_ref, x, xw, tt, ids, brow, t_o, t_m, x_s, x_r, i_s, i_r, own, own_i, *rest):
     R, B, nb_all = dims
     Z = B // 2
     r = lax.axis_index("row")
@@ -237,12 +238,12 @@
                 brow[:, at] = select(mid_t, (k - nblk_o, e), each, mrows, 1, (kl, 128))
     scale = w_ref[:, pl.ds(pl.multiple_of(r * cq, 128), cq)] * (1.0 / nb_all)
 
-    n = len(rest) // 2
-    last = nblk - 1
-    ab = Stream(rest[:n], [(i, j) for i in range(last) for j in range(i, last)], True, core, pair_dev,
-                ((Z, zi, z_dev), (R, r, row_dev)))
-    bb = Stream(rest[n:], [(i, last) for i in range(nblk)], False, core, pair_dev,
-                ((R, r, row_dev), (Z, zi, z_dev)))
+    z_axis, row_axis = (Z, zi, z_dev), (R, r, row_dev)
+    n = len(rest) // 3
+    s1, s2, s3 = [
+        Stream(rest[i * n:(i + 1) * n], blocks, z_first, core, pair_dev,
+               (z_axis, row_axis) if z_first else (row_axis, z_axis))
+        for i, (blocks, z_first) in enumerate(plan(nblk))]
 
     def arrive(k):
         for c in chunks[k]:
@@ -250,23 +251,22 @@
         rows = slice(k * BLK, (k + 1) * BLK)
         v = x[rows, :].astype(F32) * scale
         h = v.astype(BF16)
-        xh[rows, :] = h
-        xl[rows, :] = (v - h.astype(F32)).astype(BF16)
-
-    for k in range(last):
-        arrive(k)
-    ab.compute(x, xh, xl)
-    ab.pair_start()
-    ab.one_start()
-    arrive(last)
-    bb.compute(x, xh, xl)
-    bb.pair_start()
-    bb.one_start()
-    ab.two_start()
-    bb.two_start()
-    ab.back_start()
-    bb.back_start()
-    ab.spread_rest()
+        xw[k, :BLK, :] = h
+        xw[k, BLK:, :] = (v - h.astype(F32)).astype(BF16)
+
+    for stream in (s1, s2, s3):
+        for k in stream.blocks:
+            arrive(k)
+        stream.compute(x, xw)
+        stream.pair_start()
+        stream.one_start()
+    s1.two_start()
+    s3.two_start()
+    s2.two_start()
+    s1.back_start()
+    s3.back_start()
+    s2.back_start()
+    s1.spread_rest()
 
     for c in id_copies:
         c.wait()
@@ -278,35 +278,56 @@
     bcol = [select(oid_c, (k, 0), each, orows, 0, (BLK, kc)) for k in range(nblk_o)]
     bcol += [select(mid_c, (k, 0), each, mrows, 0, (BLK, kc)) for k in range(nblk_m)]
 
-    t_m = [jnp.zeros((BLK, kc), F32) for _ in range(nblk)]
-    t_o = [jnp.zeros((BLK, kc), F32) for _ in range(nblk)]
+    t_o[...] = jnp.zeros_like(t_o)
+    t_m[...] = jnp.zeros_like(t_m)
+    cut = nblk_o * BLK
+
+    def times(v, cols_of):
+        total = None
+        for p in split3(v):
+            total = dot(p, cols_of) if total is None else total + dot(p, cols_of)
+        return total
 
     def gather(stream):
         stream.wait()
-        for k, (i, j) in enumerate(stream.blocks):
-            g = stream.full[k * BLK:(k + 1) * BLK, :]
-            for to, frm, part in ((i, j, g), (j, i, g.T)) if i != j else ((i, j, g),):
-                here = t_o if frm < nblk_o else t_m
-                for p in split3(part):
-                    here[to] = here[to] + dot(p, bcol[frm])
-
-    bb.spread_rest()
-    ab.pair_back()
-    gather(ab)
-    bb.pair_back()
-    gather(bb)
-    g_m = jnp.zeros((kl, kc), F32)
-    g_o = jnp.zeros((kl, kc), F32)
-    for i in range(nblk):
-        s = brow[:, i * BLK:(i + 1) * BLK]
-        acc = jnp.zeros((kl, kc), F32)
-        for p in split3(t_m[i] + t_o[i] * c_col):
-            acc = acc + dot(s, p)
-        if i < nblk_o:
-            g_o = g_o + acc
-        else:
-            g_m = g_m + acc
+        at = 0
+        for k in stream.blocks:
+            m = (k + 1) * BLK
+            strip = stream.full[at:at + m, :]
+            at += m
+            t = t_o if k < nblk_o else t_m
+            t[:m, :] = t[:m, :] + times(strip, bcol[k])
+            rows = slice(k * BLK, m)
+            above = min(k * BLK, cut)
+            if above > 0:
+                part = jnp.concatenate(bcol[:above // BLK], axis=0)
+                t_o[rows, :] = t_o[rows, :] + times(strip[:above, :].T, part)
+            if k * BLK > cut:
+                part = jnp.concatenate(bcol[nblk_o:k], axis=0)
+                t_m[rows, :] = t_m[rows, :] + times(strip[cut:k * BLK, :].T, part)
+
+    s1.pair_back()
+    s3.spread_rest()
+    s2.spread_rest()
+    gather(s1)
+    s3.pair_back()
+    gather(s3)
+    s2.pair_back()
+    gather(s2)
+    t = t_m[...] + t_o[...] * c_col
+    g_o = times_left(brow[:, :cut], t[:cut, :])
+    g_m = times_left(brow[:, cut:], t[cut:, :])
     gram_ref[...] = g_m + g_o * jnp.concatenate([c_row] * (kc // 128), axis=1)
+
+
+def times_left(s, v):
+    a, b, c = split3(v)
+    return dot(s, a) + dot(s, b) + dot(s, c)
+
+
+def plan(nblk):
+    half = nblk // 2
+    return ((range(half), True), (range(half, nblk - 1), True), (range(nblk - 1, nblk), False))
 
 
 def solution(mesh):
@@ -354,15 +375,19 @@
             out_specs=vmem,
             scratch_shapes=[
                 pltpu.VMEM((n, cq), BF16),
-                pltpu.VMEM((n, cq), BF16),
-                pltpu.VMEM((n, cq), BF16),
+                pltpu.VMEM((nblk, 2 * BLK, cq), BF16),
                 pltpu.VMEM((lodf_table.shape[0], 128), F32),
                 pltpu.VMEM((3, R, 1, kl), jnp.int32),
                 pltpu.VMEM((kl, n), BF16),
+                pltpu.VMEM((n, kc), F32),
+                pltpu.VMEM((n, kc), F32),
                 dma((R - 1, nblk)), dma((R - 1, nblk)),
                 dma((3, R - 1)), dma((3, R - 1)),
                 dma((nblk,)), dma((3,)),
-            ] + stream_scratch(nblk * (nblk - 1) // 2, Z, R) + stream_scratch(nblk, R, Z),
+            ] + [
+                ref for blocks, z_first in plan(nblk)
+                for ref in stream_scratch(sum(k + 1 for k in blocks), *((Z, R) if z_first else (R, Z)))
+            ],
             compiler_params=pltpu.CompilerParams(
                 collective_id=0, has_side_effects=True, vmem_limit_bytes=60 * 1024 * 1024),
         )(monitored, outaged, bus_weight[None, :], lodf_table[None, :],

time: 55.9 us -> 57.3 us (1.025)
  Pallas kernels: 53.8 us -> 55.2 us
    pallas_call x1, Pallas kernels: 53.8 us -> 55.2 us  [local(): pl.pallas_call(functools.partial(kernel, (R, B, cols * B)), out_shape=jax...]
where the time goes in v3:
time: 57.3 us; the launch traced here: 57.1 us
  Pallas kernels  55.2 us (96%)
  local copies, waits for them, and re-layouts  1.87 us (3%)
    pallas_call x1, Pallas kernels, local(): pl.pallas_call(functools.partial(kernel, (R, B, cols * B)), out_shape=jax...  55.2 us
    unnamed x1, local copies, waits for them, and re-layouts  1.87 us

profile of v3, /device:TPU:0, one launch (start us, length us, event | category | flops | bytes accessed | tf_op | source)
XLA Modules:
  0.0 57.1 jit_solution(5030127386619856630)
XLA Ops:
  0.0 55.2 %shard_map.73 = f32[512,256]{1,0:T(8,128)} custom-call(bf16[128,4096]{1,0:T(8,128)(2,1)} %mon_ref.1, bf16[64,4096]{1,0:T(8,128)(2,1)} %out_ref.1, f32[1,4096]{1,0:T(1,128)} %bitcast.5, f32[1,1024]{1,0:T(1,128)} %bitcast.6, s32[1,512]{1,0:T(1,128)} %bitcast.7, s32[1,512]{1,0:T(1,128)} %bitcast.8, s32[1,512]{1,0:T(1,128)} %bitcast.9), custom_call_target="tpu_custom_call" | custom-call | tf_op jit(solution)/shard_map/pallas_call | solution.py:371
  55.2 1.9 %copy.9 = f32[512,256]{1,0:T(8,128)} copy(f32[512,256]{1,0:T(8,128)} %shard_map.73) | data formatting | bytes 1048576

commit v4 on v3

--- a/solution.py
+++ b/solution.py
@@ -13,11 +13,9 @@
 MESH = pl.DeviceIdType.MESH
 
 
-def split3(v):
+def split(v):
     a = v.astype(BF16)
-    rest = v - a.astype(F32)
-    b = rest.astype(BF16)
-    return a, b, (rest - b.astype(F32)).astype(BF16)
+    return a, (v - a.astype(F32)).astype(BF16)
 
 
 def dot(a, b):
@@ -158,8 +156,8 @@
     return jnp.where(ids == line + block[0] * rows_each, 1.0, 0.0).astype(BF16)
 
 
-def kernel(dims, mon_ref, out_ref, w_ref, table_ref, mid_ref, oid_ref, lid_ref,
-           gram_ref, x, xw, tt, ids, brow, t_o, t_m, x_s, x_r, i_s, i_r, own, own_i, *rest):
+def kernel(dims, mon_ref, out_ref, w_hbm, table_hbm, mid_hbm, oid_hbm, lid_hbm,
+           gram_ref, w_ref, table_ref, mid_ref, oid_ref, lid_ref, small, x, xw, tt, ids, brow, t_o, t_m, x_s, x_r, i_s, i_r, own, own_i, *rest):
     R, B, nb_all = dims
     Z = B // 2
     r = lax.axis_index("row")
@@ -174,6 +172,12 @@
     nblk = nblk_m + nblk_o
     kl = mid_ref.shape[1]
     kc = kl * R // B
+    loads = []
+    for i, (src, dst) in enumerate(((w_hbm, w_ref), (table_hbm, table_ref), (mid_hbm, mid_ref),
+                                    (oid_hbm, oid_ref), (lid_hbm, lid_ref))):
+        c = pltpu.make_async_copy(src, dst, small.at[i])
+        c.start()
+        loads.append(c)
 
     def row_dev(q):
         return {"row": q}
@@ -211,6 +215,8 @@
         c.start()
         chunk.append(c)
         chunks.append(chunk)
+    for c in loads:
+        c.wait()
     id_copies = []
     for i, src in enumerate((mid_ref, oid_ref, lid_ref)):
         for d in range(1, R):
@@ -259,14 +265,15 @@
             arrive(k)
         stream.compute(x, xw)
         stream.pair_start()
+        if stream is s3:
+            s1.two_start()
         stream.one_start()
-    s1.two_start()
+    s1.back_start()
     s3.two_start()
     s2.two_start()
-    s1.back_start()
+    s1.spread_rest()
     s3.back_start()
     s2.back_start()
-    s1.spread_rest()
 
     for c in id_copies:
         c.wait()
@@ -284,7 +291,7 @@
 
     def times(v, cols_of):
         total = None
-        for p in split3(v):
+        for p in split(v):
             total = dot(p, cols_of) if total is None else total + dot(p, cols_of)
         return total
 
@@ -321,8 +328,8 @@
 
 
 def times_left(s, v):
-    a, b, c = split3(v)
-    return dot(s, a) + dot(s, b) + dot(s, c)
+    a, b = split(v)
+    return dot(s, a) + dot(s, b)
 
 
 def plan(nblk):
@@ -371,9 +378,15 @@
         return pl.pallas_call(
             functools.partial(kernel, (R, B, cols * B)),
             out_shape=jax.ShapeDtypeStruct((kl, kc), F32),
-            in_specs=[hbm, hbm] + [vmem] * 5,
+            in_specs=[hbm] * 7,
             out_specs=vmem,
             scratch_shapes=[
+                pltpu.VMEM((1, cols), F32),
+                pltpu.VMEM((1, lodf_table.shape[0]), F32),
+                pltpu.VMEM((1, kl), jnp.int32),
+                pltpu.VMEM((1, kl), jnp.int32),
+                pltpu.VMEM((1, kl), jnp.int32),
+                dma((5,)),
                 pltpu.VMEM((n, cq), BF16),
                 pltpu.VMEM((nblk, 2 * BLK, cq), BF16),
                 pltpu.VMEM((lodf_table.shape[0], 128), F32),

time: 57.3 us -> 54.4 us (0.949)
  Pallas kernels: 55.2 us -> 52.4 us
    pallas_call x1, Pallas kernels: 55.2 us -> 52.4 us  [local(): pl.pallas_call(functools.partial(kernel, (R, B, cols * B)), out_shape=jax...]
where the time goes in v4:
time: 54.4 us; the launch traced here: 54.2 us
  Pallas kernels  52.4 us (96%)
  local copies, waits for them, and re-layouts  1.87 us (3%)
    pallas_call x1, Pallas kernels, local(): pl.pallas_call(functools.partial(kernel, (R, B, cols * B)), out_shape=jax...  52.4 us
    unnamed x1, local copies, waits for them, and re-layouts  1.87 us

profile of v4, /device:TPU:0, one launch (start us, length us, event | category | flops | bytes accessed | tf_op | source)
XLA Modules:
  0.0 54.2 jit_solution(3626075228141557270)
XLA Ops:
  0.0 52.4 %shard_map.73 = f32[512,256]{1,0:T(8,128)} custom-call(bf16[128,4096]{1,0:T(8,128)(2,1)} %mon_ref.1, bf16[64,4096]{1,0:T(8,128)(2,1)} %out_ref.1, f32[1,4096]{1,0:T(1,128)} %bitcast.5, f32[1,1024]{1,0:T(1,128)} %bitcast.6, s32[1,512]{1,0:T(1,128)} %bitcast.7, s32[1,512]{1,0:T(1,128)} %bitcast.8, s32[1,512]{1,0:T(1,128)} %bitcast.9), custom_call_target="tpu_custom_call" | custom-call | tf_op jit(solution)/shard_map/pallas_call | solution.py:378
  52.4 1.9 %copy.9 = f32[512,256]{1,0:T(8,128)} copy(f32[512,256]{1,0:T(8,128)} %shard_map.73) | data formatting | bytes 1048576

commit v5 on v4

--- a/solution.py
+++ b/solution.py
@@ -45,7 +45,7 @@
 
 
 class Stream:
-    def __init__(self, refs, blocks, me, core, other, axes):
+    def __init__(self, refs, blocks, z_first, z_back, core, other, axes):
         (self.gp, self.cbuf, self.acc, self.b1, self.s1, self.b2, self.full,
          self.cs, self.cr, self.p1s, self.p1r, self.p2s, self.p2r,
          self.a1s, self.a1r, self.a2s, self.a2r, self.ds, self.dr) = refs
@@ -55,7 +55,7 @@
         self.H = self.gp.shape[0] // 2
         self.h1 = self.H // self.n1
         self.pz = self.h1 // self.n2
-        self.z_first = me
+        self.z_first, self.z_back = z_first, z_back
 
     def compute(self, x, xw):
         at = 0
@@ -114,30 +114,31 @@
         total = self.s1[self.rows(self.i2 * self.pz, self.pz), :]
         for d in range(1, self.n2):
             total = total + self.b2[d - 1]
-        if self.z_first:
-            self.Z, self.zi, self.zdev = self.n1, self.i1, self.dev1
-            self.R, self.r, self.rdev = self.n2, self.i2, self.dev2
-        else:
-            self.Z, self.zi, self.zdev = self.n2, self.i2, self.dev2
-            self.R, self.r, self.rdev = self.n1, self.i1, self.dev1
-        at = self.piece(self.zi, self.r)
+        one, two = (self.n1, self.i1, self.dev1), (self.n2, self.i2, self.dev2)
+        if self.z_first != self.z_back:
+            one, two = two, one
+        (self.m1, self.k1, self.to1), (self.m2, self.k2, self.to2) = one, two
+        at = self.back_piece(self.k1)
         self.full[at, :] = total
         ref = self.full.at[at, :]
         self.zc = []
-        for d in range(1, self.Z):
+        for d in range(1, self.m1):
             self.zc.append(self.send(ref, ref, self.a1s.at[d - 1], self.a1r.at[d - 1],
-                                     self.zdev(lax.rem(self.zi + d, self.Z))))
+                                     self.to1(lax.rem(self.k1 + d, self.m1))))
         self.c = []
         self.spread(0)
 
+    def back_piece(self, k):
+        return self.piece(k, self.k2) if self.z_back else self.piece(self.k2, k)
+
     def spread(self, e):
-        ref = self.full.at[self.piece(lax.rem(self.zi + self.Z - e, self.Z), self.r), :]
-        for d in range(1, self.R):
+        ref = self.full.at[self.back_piece(lax.rem(self.k1 + self.m1 - e, self.m1)), :]
+        for d in range(1, self.m2):
             self.c.append(self.send(ref, ref, self.a2s.at[e, d - 1], self.a2r.at[e, d - 1],
-                                    self.rdev(lax.rem(self.r + d, self.R))))
+                                    self.to2(lax.rem(self.k2 + d, self.m2))))
 
     def spread_rest(self):
-        for e in range(1, self.Z):
+        for e in range(1, self.m1):
             self.zc[e - 1].wait()
             self.spread(e)
 
@@ -247,9 +248,9 @@
     z_axis, row_axis = (Z, zi, z_dev), (R, r, row_dev)
     n = len(rest) // 3
     s1, s2, s3 = [
-        Stream(rest[i * n:(i + 1) * n], blocks, z_first, core, pair_dev,
+        Stream(rest[i * n:(i + 1) * n], blocks, z_first, z_back, core, pair_dev,
                (z_axis, row_axis) if z_first else (row_axis, z_axis))
-        for i, (blocks, z_first) in enumerate(plan(nblk))]
+        for i, (blocks, z_first, z_back) in enumerate(plan(nblk))]
 
     def arrive(k):
         for c in chunks[k]:
@@ -313,13 +314,13 @@
                 part = jnp.concatenate(bcol[nblk_o:k], axis=0)
                 t_m[rows, :] = t_m[rows, :] + times(strip[cut:k * BLK, :].T, part)
 
-    s1.pair_back()
     s3.spread_rest()
     s2.spread_rest()
+    s1.pair_back()
+    s3.pair_back()
     gather(s1)
-    s3.pair_back()
+    s2.pair_back()
     gather(s3)
-    s2.pair_back()
     gather(s2)
     t = t_m[...] + t_o[...] * c_col
     g_o = times_left(brow[:, :cut], t[:cut, :])
@@ -334,14 +335,15 @@
 
 def plan(nblk):
     half = nblk // 2
-    return ((range(half), True), (range(half, nblk - 1), True), (range(nblk - 1, nblk), False))
+    return ((range(half), True, False), (range(half, nblk - 1), True, True),
+            (range(nblk - 1, nblk), False, True))
 
 
 def solution(mesh):
     R, B = mesh.shape["row"], mesh.shape["bus"]
     Z = B // 2
 
-    def stream_scratch(blocks, n1, n2):
+    def stream_scratch(blocks, n1, n2, m1, m2):
         unit = 8 * R * B
         packed = -(-(blocks * BLK) // unit) * unit
         H = packed // 2
@@ -359,8 +361,8 @@
             dma, dma,
             dma((n1 - 1,)), dma((n1 - 1,)),
             dma((n2 - 1,)), dma((n2 - 1,)),
-            dma((Z - 1,)), dma((Z - 1,)),
-            dma((Z, R - 1)), dma((Z, R - 1)),
+            dma((m1 - 1,)), dma((m1 - 1,)),
+            dma((m1, m2 - 1)), dma((m1, m2 - 1)),
             dma, dma,
         ]
 
@@ -398,8 +400,9 @@
                 dma((3, R - 1)), dma((3, R - 1)),
                 dma((nblk,)), dma((3,)),
             ] + [
-                ref for blocks, z_first in plan(nblk)
-                for ref in stream_scratch(sum(k + 1 for k in blocks), *((Z, R) if z_first else (R, Z)))
+                ref for blocks, z_first, z_back in plan(nblk)
+                for ref in stream_scratch(sum(k + 1 for k in blocks), *((Z, R) if z_first else (R, Z)),
+                                          *((Z, R) if z_back else (R, Z)))
             ],
             compiler_params=pltpu.CompilerParams(
                 collective_id=0, has_side_effects=True, vmem_limit_bytes=60 * 1024 * 1024),

time: 54.4 us -> 55 us (1.011)
  Pallas kernels: 52.4 us -> 53 us
    pallas_call x1, Pallas kernels: 52.4 us -> 53 us  [local(): pl.pallas_call(functools.partial(kernel, (R, B, cols * B)), out_shape=jax...]
where the time goes in v5:
time: 55 us; the launch traced here: 54.9 us
  Pallas kernels  53 us (96%)
  local copies, waits for them, and re-layouts  1.87 us (3%)
    pallas_call x1, Pallas kernels, local(): pl.pallas_call(functools.partial(kernel, (R, B, cols * B)), out_shape=jax...  53 us
    unnamed x1, local copies, waits for them, and re-layouts  1.87 us

profile of v5, /device:TPU:0, one launch (start us, length us, event | category | flops | bytes accessed | tf_op | source)
XLA Modules:
  0.0 54.9 jit_solution(6555096179142860060)
XLA Ops:
  0.0 53.0 %shard_map.73 = f32[512,256]{1,0:T(8,128)} custom-call(bf16[128,4096]{1,0:T(8,128)(2,1)} %mon_ref.1, bf16[64,4096]{1,0:T(8,128)(2,1)} %out_ref.1, f32[1,4096]{1,0:T(1,128)} %bitcast.5, f32[1,1024]{1,0:T(1,128)} %bitcast.6, s32[1,512]{1,0:T(1,128)} %bitcast.7, s32[1,512]{1,0:T(1,128)} %bitcast.8, s32[1,512]{1,0:T(1,128)} %bitcast.9), custom_call_target="tpu_custom_call" | custom-call | tf_op jit(solution)/shard_map/pallas_call | solution.py:380
  53.0 1.9 %copy.9 = f32[512,256]{1,0:T(8,128)} copy(f32[512,256]{1,0:T(8,128)} %shard_map.73) | data formatting | bytes 1048576

commit v6 on v4

--- a/solution.py
+++ b/solution.py
@@ -245,8 +245,8 @@
     scale = w_ref[:, pl.ds(pl.multiple_of(r * cq, 128), cq)] * (1.0 / nb_all)
 
     z_axis, row_axis = (Z, zi, z_dev), (R, r, row_dev)
-    n = len(rest) // 3
-    s1, s2, s3 = [
+    n = len(rest) // 2
+    s1, s2 = [
         Stream(rest[i * n:(i + 1) * n], blocks, z_first, core, pair_dev,
                (z_axis, row_axis) if z_first else (row_axis, z_axis))
         for i, (blocks, z_first) in enumerate(plan(nblk))]
@@ -260,20 +260,17 @@
         xw[k, :BLK, :] = h
         xw[k, BLK:, :] = (v - h.astype(F32)).astype(BF16)
 
-    for stream in (s1, s2, s3):
+    for stream in (s1, s2):
         for k in stream.blocks:
             arrive(k)
         stream.compute(x, xw)
         stream.pair_start()
-        if stream is s3:
-            s1.two_start()
         stream.one_start()
+    s1.two_start()
+    s2.two_start()
     s1.back_start()
-    s3.two_start()
-    s2.two_start()
+    s2.back_start()
     s1.spread_rest()
-    s3.back_start()
-    s2.back_start()
 
     for c in id_copies:
         c.wait()
@@ -313,12 +310,9 @@
                 part = jnp.concatenate(bcol[nblk_o:k], axis=0)
                 t_m[rows, :] = t_m[rows, :] + times(strip[cut:k * BLK, :].T, part)
 
+    s2.spread_rest()
     s1.pair_back()
-    s3.spread_rest()
-    s2.spread_rest()
     gather(s1)
-    s3.pair_back()
-    gather(s3)
     s2.pair_back()
     gather(s2)
     t = t_m[...] + t_o[...] * c_col
@@ -333,8 +327,8 @@
 
 
 def plan(nblk):
-    half = nblk // 2
-    return ((range(half), True), (range(half, nblk - 1), True), (range(nblk - 1, nblk), False))
+    early = nblk - nblk // 3
+    return (range(early), True), (range(early, nblk), False)
 
 
 def solution(mesh):

time: 54.4 us -> 54 us (level)
  no operation moved by 1% of the time
where the time goes in v6:
time: 54 us; the launch traced here: 53.9 us
  Pallas kernels  52 us (96%)
  local copies, waits for them, and re-layouts  1.87 us (3%)
    pallas_call x1, Pallas kernels, local(): pl.pallas_call(functools.partial(kernel, (R, B, cols * B)), out_shape=jax...  52 us
    unnamed x1, local copies, waits for them, and re-layouts  1.87 us

profile of v6, /device:TPU:0, one launch (start us, length us, event | category | flops | bytes accessed | tf_op | source)
XLA Modules:
  0.0 53.9 jit_solution(4250015887655109313)
XLA Ops:
  0.0 52.0 %shard_map.73 = f32[512,256]{1,0:T(8,128)} custom-call(bf16[128,4096]{1,0:T(8,128)(2,1)} %mon_ref.1, bf16[64,4096]{1,0:T(8,128)(2,1)} %out_ref.1, f32[1,4096]{1,0:T(1,128)} %bitcast.5, f32[1,1024]{1,0:T(1,128)} %bitcast.6, s32[1,512]{1,0:T(1,128)} %bitcast.7, s32[1,512]{1,0:T(1,128)} %bitcast.8, s32[1,512]{1,0:T(1,128)} %bitcast.9), custom_call_target="tpu_custom_call" | custom-call | tf_op jit(solution)/shard_map/pallas_call | solution.py:372
  52.0 1.9 %copy.9 = f32[512,256]{1,0:T(8,128)} copy(f32[512,256]{1,0:T(8,128)} %shard_map.73) | data formatting | bytes 1048576
